TPU v7x, 32 devices: a whole 2x2x4 slice. The times are simulated.
32 devices in a mesh: depth: 4 (over z), row: 4 (over x, core), col: 2 (over y).
Axes of the slice: x: 2, y: 2, z: 4, core: 2. Of those that a mesh axis runs over, the one named last changes fastest.
Arguments:
- acts: bfloat16 [2048, 4096], P(('depth', 'col'), 'row'), may hold values from -0.3125 to 0.3125
- grad_out: bfloat16 [2048, 14336], P(('depth', 'row'), 'col'), may hold values from -6 to 6
- weight: bfloat16 [4096, 14336], P('row', 'col'), may hold values from -0.046875 to 0.046875
Outputs:
- grad_acts: bfloat16 [2048, 4096], P(('depth', 'col'), 'row')
- grad_weight: bfloat16 [4096, 14336], P('row', 'col')
All inputs are finite; a program needn't handle non-finite values.
Results may differ from a plain program's by a relative error of at most 0.013.
Values may be sent and summed in bfloat16 or wider, within the bound.
A program may use at most 128 MiB of HBM per device.

v0:
```python
import jax
import jax.numpy as jnp
from jax import lax
from jax.sharding import PartitionSpec as P


def shards(acts, grad_out, weight):
    grad_rows = lax.all_gather(grad_out, "row", axis=0, tiled=True)
    grad_acts = lax.psum_scatter(
        lax.dot_general(
            grad_rows, weight, (((1,), (1,)), ((), ())), preferred_element_type=jnp.float32
        ).astype(jnp.bfloat16),
        "col",
        scatter_dimension=0,
        tiled=True,
    )
    partial_sum = lax.dot_general(
        lax.all_gather(acts, "col", axis=0, tiled=True),
        grad_rows,
        (((0,), (0,)), ((), ())),
        preferred_element_type=jnp.float32,
    )
    grad_weight = lax.psum(partial_sum.astype(jnp.bfloat16), "depth")
    return (grad_acts, grad_weight)


def solution(mesh):
    in_specs = (P(("depth", "col"), "row"), P(("depth", "row"), "col"), P("row", "col"))
    out_specs = (P(("depth", "col"), "row"), P("row", "col"))
    return jax.shard_map(shards, mesh=mesh, in_specs=in_specs, out_specs=out_specs, check_vma=False)
```

profile of v0, /device:TPU:0, one launch (start us, length us, event | category | flops | bytes accessed | tf_op | source)
XLA Modules:
  0.0 627.1 jit_solution(1887198143985389784)
XLA Ops:
  7.2 0.0 all-gather.3.cloned.1.call-start
  7.2 0.7 all-gather.3.cloned.1.call-update
  7.9 0.0 all-gather.5.cloned.1.call-start
  7.9 0.7 all-gather.5.cloned.1.call-update
  8.6 0.0 reduce-scatter.2.cloned.1.call-start
  8.7 55.9 %all-gather.3.cloned.1.call-done = bf16[512,7168]{1,0:T(8,128)(2,1)} async-done(((bf16[128,7168]{1,0:T(8,128)(2,1)}), bf16[512,7168]{1,0:T(8,128)(2,1)}) %all-gather.3.cloned.1.call-update) | async-done | bytes 7340048 | tf_op jit(solution)/shard_map/all_gather | solution.py:8
  64.6 14.0 %convolution_convert_fusion.1 = bf16[512,1024]{1,0:T(8,128)(2,1)} fusion(bf16[512,7168]{1,0:T(8,128)(2,1)} %all-gather.3.cloned.1.call-done, bf16[1024,7168]{1,0:T(8,128)(2,1)} %param.5), kind=kOutput, calls=%fused_computation.1 | convolution fusion | flops 7516717056 | bytes 23068672 | tf_op jit(solution)/shard_map/dot_general | solution.py:10
  78.6 0.0 reduce-scatter.2.cloned.1.call-update
  78.6 0.0 all-reduce.2.cloned.1.call-start
  78.7 8.8 %all-gather.5.cloned.1.call-done = bf16[512,1024]{1,0:T(8,128)(2,1)} async-done(((bf16[256,1024]{1,0:T(8,128)(2,1)}), bf16[512,1024]{1,0:T(8,128)(2,1)}) %all-gather.5.cloned.1.call-update) | async-done | bytes 1048592 | tf_op jit(solution)/shard_map/all_gather | solution.py:18
  87.5 13.4 %convolution_convert_fusion = bf16[1024,7168]{1,0:T(8,128)(2,1)} fusion(bf16[512,1024]{1,0:T(8,128)(2,1)} %all-gather.5.cloned.1.call-done, bf16[512,7168]{1,0:T(8,128)(2,1)} %all-gather.3.cloned.1.call-done), kind=kOutput, calls=%fused_computation | convolution fusion | flops 7523532800 | bytes 23068672 | tf_op jit(solution)/shard_map/dot_general | solution.py:17
  100.9 0.0 all-reduce.2.cloned.1.call-update
  100.9 9.8 %reduce-scatter.2.cloned.1.call-done = bf16[256,1024]{1,0:T(8,128)(2,1)} async-done(((bf16[512,1024]{1,0:T(8,128)(2,1)}), bf16[256,1024]{1,0:T(8,128)(2,1)}) %reduce-scatter.2.cloned.1.call-update) | async-done | bytes 524304 | tf_op jit(solution)/shard_map/reduce_scatter | solution.py:9
  110.7 496.7 %all-reduce.2.cloned.1.call-done = bf16[1024,7168]{1,0:T(8,128)(2,1)} async-done(((bf16[1024,7168]{1,0:T(8,128)(2,1)}), bf16[1024,7168]{1,0:T(8,128)(2,1)}) %all-reduce.2.cloned.1.call-update) | async-done | bytes 14680080 | tf_op jit(solution)/shard_map/psum | solution.py:23
  607.4 13.2 %copy.6 = bf16[1024,7168]{1,0:T(8,128)(2,1)} copy(bf16[1024,7168]{1,0:T(8,128)(2,1)} %all-reduce.2.cloned.1.call-done) | data formatting | bytes 29360128
Async XLA Ops:
  7.2 57.4 %all-gather.3.cloned.1.call-start = ((), (), s32[]{:S(2)}) async-start(), calls=%async_computation.1 | async-start | bytes 9175040 | tf_op jit(solution)/shard_map/all_gather | solution.py:8
  7.9 79.6 %all-gather.5.cloned.1.call-start = ((), (), s32[]{:S(2)}) async-start(), calls=%async_computation.3 | async-start | bytes 1572864 | tf_op jit(solution)/shard_map/all_gather | solution.py:18
  8.6 102.0 %reduce-scatter.2.cloned.1.call-start = ((), (), s32[]{:S(2)}) async-start(), calls=%async_computation.2 | async-start | bytes 1572864 | tf_op jit(solution)/shard_map/reduce_scatter | solution.py:9
  78.6 528.8 %all-reduce.2.cloned.1.call-start = ((), (), s32[]{:S(2)}) async-start(), calls=%async_computation.4 | async-start | bytes 29360128 | tf_op jit(solution)/shard_map/psum | solution.py:23
Sparse Core Ops, SparseCore 0:
  9.5 55.0 all-gather.2
  66.1 21.2 all-gather.4
  90.3 20.3 reduce-scatter.1
  113.6 493.7 all-reduce.1
where the time goes:
time: 627 us
  waiting for transfers between devices  573 us (91%)
  matrix products  27.4 us (4%)
  between operations  13.8 us (2%)
  local copies, waits for them, and re-layouts  13.2 us (2%)
    psum x1, waiting for transfers between devices, shards(): grad_weight = lax.psum(partial_sum.astype(jnp.bfloat16), 'depth')  497 us
    all_gather x1, waiting for transfers between devices, shards(): grad_rows = lax.all_gather(grad_out, 'row', axis=0, tiled=True)  55.9 us
    dot_general x1, matrix products, shards(): lax.dot_general(grad_rows, weight, (((1,), (1,)), ((), ())), preferred_el...  14 us
    dot_general x1, matrix products, shards(): lax.dot_general(lax.all_gather(acts, 'col', axis=0, tiled=True), grad_row...  13.4 us
    unnamed x1, local copies, waits for them, and re-layouts  13.2 us
  transfers between devices with their start and end apart: 4, of which 4 were waited for; matrix products, arithmetic and copies ran while one was open for 4% of the time, Pallas kernels for 0%

commit v1 on v0

--- a/solution.py
+++ b/solution.py
@@ -20,7 +20,9 @@
         (((0,), (0,)), ((), ())),
         preferred_element_type=jnp.float32,
     )
-    grad_weight = lax.psum(partial_sum.astype(jnp.bfloat16), "depth")
+    part = partial_sum.astype(jnp.bfloat16)
+    blocks = lax.all_gather(part, "depth", axis=0, tiled=False)
+    grad_weight = blocks.sum(axis=0)
     return (grad_acts, grad_weight)
 
 

time: 627 us -> 1110 us (1.77)
  waiting for transfers between devices: 573 us -> 1040 us
  other arithmetic: 0 us -> 28 us
  local copies, waits for them, and re-layouts: 13.2 us -> 0 us
    all_gather x0 -> x1, waiting for transfers between devices: none -> 960 us  [shards(): blocks = lax.all_gather(part, 'depth', axis=0, tiled=False)]
    psum x1 -> x0, waiting for transfers between devices: 497 us -> none  [shards(): grad_weight = lax.psum(partial_sum.astype(jnp.bfloat16), 'depth')]
    reduce_sum x0 -> x1, other arithmetic: none -> 28 us  [shards(): grad_weight = blocks.sum(axis=0)]
    all_gather x1, waiting for transfers between devices: 8.8 us -> 24.9 us  [shards(): lax.all_gather(acts, 'col', axis=0, tiled=True)]
    unnamed x1 -> x0, local copies, waits for them, and re-layouts: 13.2 us -> none
  transfers between devices with their start and end apart: 4 -> 4, of which waited for: 4 -> 3; matrix products, arithmetic and copies ran while one was open for 4% -> 4% of each run, Pallas kernels for 0% -> 0%
where the time goes in v1:
time: 1110 us
  waiting for transfers between devices  1040 us (94%)
  other arithmetic  28 us (3%)
  matrix products  27.4 us (2%)
  between operations  13.8 us (1%)
    all_gather x1, waiting for transfers between devices, shards(): blocks = lax.all_gather(part, 'depth', axis=0, tiled=False)  960 us
    all_gather x1, waiting for transfers between devices, shards(): grad_rows = lax.all_gather(grad_out, 'row', axis=0, tiled=True)  53.9 us
    reduce_sum x1, other arithmetic, shards(): grad_weight = blocks.sum(axis=0)  28 us
    all_gather x1, waiting for transfers between devices, shards(): lax.all_gather(acts, 'col', axis=0, tiled=True)  24.9 us
  transfers between devices with their start and end apart: 4, of which 3 were waited for; matrix products, arithmetic and copies ran while one was open for 4% of the time, Pallas kernels for 0%

profile of v1, /device:TPU:0, one launch (start us, length us, event | category | flops | bytes accessed | tf_op | source)
XLA Modules:
  0.0 1110.0 jit_solution(5795844557770253751)
XLA Ops:
  7.2 0.0 all-gather.7.cloned.1.call-start
  7.2 0.7 all-gather.7.cloned.1.call-update
  7.9 0.0 all-gather.5.cloned.1.call-start
  7.9 0.7 all-gather.5.cloned.1.call-update
  8.6 0.0 all-gather.9.cloned.1.call-start
  8.7 24.9 %all-gather.7.cloned.1.call-done = bf16[512,1024]{1,0:T(8,128)(2,1)} async-done(((bf16[256,1024]{1,0:T(8,128)(2,1)}), bf16[512,1024]{1,0:T(8,128)(2,1)}) %all-gather.7.cloned.1.call-update) | async-done | bytes 1048592 | tf_op jit(solution)/shard_map/all_gather | solution.py:18
  33.6 53.9 %all-gather.5.cloned.1.call-done = bf16[512,7168]{1,0:T(8,128)(2,1)} async-done(((bf16[128,7168]{1,0:T(8,128)(2,1)}), bf16[512,7168]{1,0:T(8,128)(2,1)}) %all-gather.5.cloned.1.call-update) | async-done | bytes 7340048 | tf_op jit(solution)/shard_map/all_gather | solution.py:8
  87.5 13.4 %convolution_convert_fusion = bf16[1024,7168]{1,0:T(8,128)(2,1)} fusion(bf16[512,1024]{1,0:T(8,128)(2,1)} %all-gather.7.cloned.1.call-done, bf16[512,7168]{1,0:T(8,128)(2,1)} %all-gather.5.cloned.1.call-done), kind=kOutput, calls=%fused_computation | convolution fusion | flops 7523532800 | bytes 23068672 | tf_op jit(solution)/shard_map/dot_general | solution.py:17
  100.9 0.0 all-gather.9.cloned.1.call-update
  100.9 0.0 reduce-scatter.2.cloned.1.call-start
  101.0 14.0 %convolution_convert_fusion.1 = bf16[512,1024]{1,0:T(8,128)(2,1)} fusion(bf16[512,7168]{1,0:T(8,128)(2,1)} %all-gather.5.cloned.1.call-done, bf16[1024,7168]{1,0:T(8,128)(2,1)} %param.5), kind=kOutput, calls=%fused_computation.1 | convolution fusion | flops 7516717056 | bytes 23068672 | tf_op jit(solution)/shard_map/dot_general | solution.py:10
  115.0 0.0 reduce-scatter.2.cloned.1.call-update
  115.0 960.5 %all-gather.9.cloned.1.call-done = bf16[4096,7168]{1,0:T(8,128)(2,1)} async-done(((bf16[1024,7168]{1,0:T(8,128)(2,1)}), bf16[4096,7168]{1,0:T(8,128)(2,1)}) %all-gather.9.cloned.1.call-update) | async-done | bytes 58720272 | tf_op jit(solution)/shard_map/all_gather | solution.py:24
  1075.5 28.0 %reduce_sum.12 = bf16[1024,7168]{1,0:T(8,128)(2,1)} reduce(bf16[4,1024,7168]{2,1,0:T(8,128)(2,1)} %bitcast.5, bf16[]{:T(256)} %constant.2.clone.1), dimensions={0}, to_apply=%region_1.0 | reduce | flops 22020096 | bytes 73400320 | tf_op jit(solution)/shard_map/reduce_sum | solution.py:25
  1103.4 0.0 reduce-scatter.2.cloned.1.call-done
Async XLA Ops:
  7.2 26.4 %all-gather.7.cloned.1.call-start = ((), (), s32[]{:S(2)}) async-start(), calls=%async_computation.3 | async-start | bytes 1572864 | tf_op jit(solution)/shard_map/all_gather | solution.py:18
  7.9 79.6 %all-gather.5.cloned.1.call-start = ((), (), s32[]{:S(2)}) async-start(), calls=%async_computation.1 | async-start | bytes 9175040 | tf_op jit(solution)/shard_map/all_gather | solution.py:8
  8.6 1066.8 %all-gather.9.cloned.1.call-start = ((), (), s32[]{:S(2)}) async-start(), calls=%async_computation.4 | async-start | bytes 73400320 | tf_op jit(solution)/shard_map/all_gather | solution.py:24
  100.9 1002.5 %reduce-scatter.2.cloned.1.call-start = ((), (), s32[]{:S(2)}) async-start(), calls=%async_computation.2 | async-start | bytes 1572864 | tf_op jit(solution)/shard_map/reduce_scatter | solution.py:9
Sparse Core Ops, SparseCore 0:
  9.5 23.9 all-gather.6
  35.1 52.2 all-gather.4
  101.0 974.3 all-gather.8
  1078.1 18.5 reduce-scatter.1
